TPU v7x, 32 devices: a whole 2x2x4 slice. The times are simulated.
32 devices in a mesh: role: 4 (over y, x), dom: 8 (over z, core).
Axes of the slice: x: 2, y: 2, z: 4, core: 2. Of those that a mesh axis runs over, the one named last changes fastest.
Arguments:
- node_feats: bfloat16 [4096, 512], P(('role', 'dom')), may hold values from -6 to 6
- hub_feats: bfloat16 [128, 512], P(('role', 'dom')), may hold values from -6 to 6
- weight: bfloat16 [1024, 512], replicated, may hold values from -0.1875 to 0.1875
- edge_src: int32 [32, 1024], P(('role', 'dom')), may hold values from 0 to 287, as said below
- edge_dst: int32 [32, 1024], P(('role', 'dom')), may hold values from 0 to 127, as said below
- bound_rows: int32 [32, 16], P(('role', 'dom')), may hold values from 0 to 127
- hub_edge_src: int32 [32, 128], P(('role', 'dom')), may hold values from 0 to 127
- hub_edge_slot: int32 [32, 128], P(('role', 'dom')), may hold values from 0 to 63, as said below
- slot_hub: int32 [32, 64], P(('role', 'dom')), may hold values from 0 to 3, as said below
Outputs:
- node_out: bfloat16 [4096, 512], P(('role', 'dom'))
- hub_out: bfloat16 [128, 512], P(('role', 'dom'))
Inputs may be any that keep to these rules, and one draw needn't show every extreme that they name: `edge_src`: row indices into the source table of the device: its own nodes, then 16 rows of the device before it along dom, then 16 of the device after it, then the 128 hubs. `edge_dst`: each node of a device is the destination of at least one of the device's edges. `hub_edge_slot`: every slot of a device receives at least one of its hub edges; slot s belongs to the owner numbered s // 2. `slot_hub`: every hub of every owner is fed by at least one slot of some device.
All inputs are finite; a program needn't handle non-finite values.
Results may differ from a plain program's by a relative error of at most 0.0027.
Values may be sent and summed in bfloat16 or wider, within the bound.
A program may use at most 64 MiB of HBM per device.

v0:
```python
import math
import jax
import jax.numpy as jnp
from jax import lax
from jax.sharding import PartitionSpec as P

epsilon = 1e-06


def extended(block, sides, width):
    for axis, dim in sides:
        count = lax.axis_size(axis)
        forward = [(i, i + 1) for i in range(count - 1)]
        forward.append((count - 1, 0))
        backward = [(target, source) for source, target in forward]
        low = lax.ppermute(
            lax.slice_in_dim(block, block.shape[dim] - width, None, axis=dim), axis, forward
        )
        high = lax.ppermute(lax.slice_in_dim(block, 0, width, axis=dim), axis, backward)
        block = jnp.concatenate([low, block, high], axis=dim)
    return block


def sage_update(self_rows, mean_rows, weight):
    feature_width = self_rows.shape[1]
    linear = jnp.dot(self_rows, weight[:feature_width], preferred_element_type=jnp.float32)
    linear = linear + jnp.dot(mean_rows, weight[feature_width:], preferred_element_type=jnp.float32)
    rectified = jnp.maximum(linear, 0.0)
    inverse_norm = lax.rsqrt(jnp.mean(rectified * rectified, axis=1, keepdims=True) + epsilon)
    return (rectified * inverse_norm).astype(jnp.bfloat16)


def on_device(
    node_feats,
    hub_feats,
    weight,
    edge_src,
    edge_dst,
    bound_rows,
    hub_edge_src,
    hub_edge_slot,
    slot_hub,
):
    feature_width = node_feats.shape[1]
    local_nodes = node_feats.shape[0]
    hub_local = hub_feats.shape[0]
    exports = node_feats[bound_rows[0]]
    bound_size = exports.shape[0]
    widened = extended(exports, (("dom", 0),), bound_size)
    hub_table = lax.all_gather(hub_feats, ("role", "dom"), axis=0, tiled=True)
    source_table = jnp.concatenate(
        [node_feats, widened[:bound_size], widened[2 * bound_size :], hub_table], axis=0
    )
    sources = edge_src[0]
    targets = edge_dst[0]
    edge_block = math.gcd(sources.shape[0], 2048)

    def add_block(sums, indices):
        node_sums, node_degree = sums
        block_sources, block_targets = indices
        picked = source_table[block_sources].astype(jnp.float32)
        return (
            (node_sums.at[block_targets].add(picked), node_degree.at[block_targets].add(1.0)),
            None,
        )

    initial = (
        jnp.zeros((local_nodes, feature_width), jnp.float32),
        jnp.zeros((local_nodes,), jnp.float32),
    )
    (node_sums, node_degree), unused = lax.scan(
        add_block, initial, (sources.reshape(-1, edge_block), targets.reshape(-1, edge_block))
    )
    hub_sources = hub_edge_src[0]
    hub_slots = hub_edge_slot[0]
    slot_table = slot_hub[0]
    slot_total = slot_table.shape[0]
    role_count = lax.axis_size("role")
    dom_count = lax.axis_size("dom")
    per_owner = slot_total // (role_count * dom_count)
    partial_value = (
        jnp.zeros((slot_total, feature_width), jnp.float32)
        .at[hub_slots]
        .add(node_feats[hub_sources].astype(jnp.float32))
    )
    slot_counts = jnp.zeros((slot_total,), jnp.float32).at[hub_slots].add(1.0)
    outgoing = (
        partial_value.reshape(role_count, dom_count, per_owner, feature_width),
        slot_counts.reshape(role_count, dom_count, per_owner),
        slot_table.astype(jnp.float32).reshape(role_count, dom_count, per_owner),
    )
    incoming_rows, incoming_counts, incoming_hubs = (
        lax.all_to_all(
            lax.all_to_all(outgoing[0], "role", split_axis=0, concat_axis=0, tiled=True),
            "dom",
            split_axis=1,
            concat_axis=1,
            tiled=True,
        ),
        lax.all_to_all(
            lax.all_to_all(outgoing[1], "role", split_axis=0, concat_axis=0, tiled=True),
            "dom",
            split_axis=1,
            concat_axis=1,
            tiled=True,
        ),
        lax.all_to_all(
            lax.all_to_all(outgoing[2], "role", split_axis=0, concat_axis=0, tiled=True),
            "dom",
            split_axis=1,
            concat_axis=1,
            tiled=True,
        ),
    )
    incoming_rows = incoming_rows.reshape(-1, feature_width)
    onehot = (
        incoming_hubs.reshape(-1)[:, None] == jnp.arange(hub_local, dtype=jnp.float32)[None, :]
    ).astype(jnp.float32)
    hub_sums = jnp.dot(
        onehot.T, incoming_rows, precision=lax.Precision.HIGHEST, preferred_element_type=jnp.float32
    )
    hub_degree = jnp.dot(
        incoming_counts.reshape(-1),
        onehot,
        precision=lax.Precision.HIGHEST,
        preferred_element_type=jnp.float32,
    )
    node_mean = (node_sums / node_degree[:, None]).astype(jnp.bfloat16)
    node_out = sage_update(node_feats, node_mean, weight)
    hub_mean = (hub_sums / hub_degree[:, None]).astype(jnp.bfloat16)
    hub_out = sage_update(hub_feats, hub_mean, weight)
    return (node_out, hub_out)


def solution(mesh):
    return jax.shard_map(
        on_device,
        mesh=mesh,
        in_specs=(
            P(("role", "dom"), None),
            P(("role", "dom"), None),
            P(),
            P(("role", "dom"), None),
            P(("role", "dom"), None),
            P(("role", "dom"), None),
            P(("role", "dom"), None),
            P(("role", "dom"), None),
            P(("role", "dom"), None),
        ),
        out_specs=(P(("role", "dom"), None), P(("role", "dom"), None)),
        check_vma=False,
    )
```

profile of v0, /device:TPU:0, one launch (start us, length us, event | category | flops | bytes accessed | tf_op | source)
XLA Modules:
  0.0 118.5 jit_solution(10749074931665273671)
XLA Ops:
  0.6 0.0 copy-start
  0.6 0.0 copy-start.1
  0.7 0.0 copy-start.2
  0.7 0.7 fusion.18
  1.5 1.5 %gather_fusion = bf16[16,512]{1,0:T(8,128)(2,1)S(1)} fusion(bf16[128,512]{1,0:T(8,128)(2,1)} %param.9, s32[1024]{0:T(1024)S(1)} %pad_clamp_fusion.1), kind=kCustom, calls=%fused_computation | custom fusion | bytes 32832 | tf_op jit(solution)/shard_map/gather | solution.py:47
  3.0 0.5 collective-permute-start
  3.5 4.1 %collective-permute-start.1 = (bf16[16,512]{1,0:T(8,128)(2,1)S(1)}, bf16[16,512]{1,0:T(8,128)(2,1)S(1)}, u32[]{:S(2)}, u32[]{:S(2)}) collective-permute-start(bf16[16,512]{1,0:T(8,128)(2,1)S(1)} %gather_fusion), channel_id=1, source_target_pairs={{1,0},{2,1},{3,2},{4,3},{5,4},{6,5},{7,6},{0,7},{9,8},{10,9},{11,1... | collective-permute-start | bytes 49160 | tf_op jit(solution)/shard_map/ppermute | solution.py:19
  7.6 0.7 fusion.19
  8.3 1.4 %scatter_custom_fusion.3 = f32[64]{0:T(128)S(1)} fusion(s32[128]{0:T(128)S(1)} %fusion.19, f32[128]{0:T(128)S(1)} %broadcast.143, f32[]{:T(128)} %constant.9.clone.1), kind=kCustom, calls=%fused_computation.50 | custom fusion | flops 128 | bytes 260 | tf_op jit(solution)/shard_map/scatter-add | solution.py:86
  9.7 0.1 reshape.180
  9.8 0.7 copy.22
  10.5 4.2 %all-to-all-start.4 = ((f32[4,8,2]{1,2,0:T(2,128)}), f32[4,8,2]{1,2,0:T(2,128)S(1)}, u32[]{:S(2)}, u32[]{:S(2)}) async-start(f32[4,8,2]{1,2,0:T(2,128)} %copy.22), calls=%async_computation.4 | async-start | bytes 8192 | tf_op jit(solution)/shard_map/all_to_all | solution.py:101
  14.6 1.3 %fusion.9 = f32[128,512]{1,0:T(8,128)S(1)} fusion(bf16[128,512]{1,0:T(8,128)(2,1)} %param.9, bf16[1024,512]{1,0:T(8,128)(2,1)} %param.11), kind=kOutput, calls=%fused_computation.20 | convolution fusion | flops 67108864 | bytes 917504 | tf_op jit(solution)/shard_map/dot_general | solution.py:26
  16.0 0.9 fusion.7
  16.9 0.1 convert_element_type.31
  17.1 0.7 copy.17
  17.7 1.6 %all-to-all-done.4 = f32[4,8,2]{1,2,0:T(2,128)S(1)} async-done(((f32[4,8,2]{1,2,0:T(2,128)}), f32[4,8,2]{1,2,0:T(2,128)S(1)}, u32[]{:S(2)}, u32[]{:S(2)}) %all-to-all-start.4) | async-done | bytes 288 | tf_op jit(solution)/shard_map/all_to_all | solution.py:101
  19.3 3.2 %all-to-all-start = ((f32[4,8,2]{1,2,0:T(2,128)}), f32[4,8,2]{1,2,0:T(2,128)S(1)}, u32[]{:S(2)}, u32[]{:S(2)}) async-start(f32[4,8,2]{1,2,0:T(2,128)} %copy.17), calls=%async_computation | async-start | bytes 8192 | tf_op jit(solution)/shard_map/all_to_all | solution.py:108
  22.6 0.7 copy.23
  23.3 3.9 %all-to-all-done = f32[4,8,2]{1,2,0:T(2,128)S(1)} async-done(((f32[4,8,2]{1,2,0:T(2,128)}), f32[4,8,2]{1,2,0:T(2,128)S(1)}, u32[]{:S(2)}, u32[]{:S(2)}) %all-to-all-start) | async-done | bytes 288 | tf_op jit(solution)/shard_map/all_to_all | solution.py:108
  27.2 3.3 %all-to-all-start.5 = ((f32[4,8,2]{0,2,1:T(2,128)}), f32[4,8,2]{0,2,1:T(2,128)S(1)}, u32[]{:S(2)}, u32[]{:S(2)}) async-start(f32[4,8,2]{0,2,1:T(2,128)} %copy.23), calls=%async_computation.5 | async-start | bytes 16384 | tf_op jit(solution)/shard_map/all_to_all | solution.py:100
  30.6 0.7 copy.18
  31.3 4.8 %all-to-all-done.5 = f32[4,8,2]{0,2,1:T(2,128)S(1)} async-done(((f32[4,8,2]{0,2,1:T(2,128)}), f32[4,8,2]{0,2,1:T(2,128)S(1)}, u32[]{:S(2)}, u32[]{:S(2)}) %all-to-all-start.5) | async-done | bytes 288 | tf_op jit(solution)/shard_map/all_to_all | solution.py:100
  36.1 3.3 %all-to-all-start.1 = ((f32[4,8,2]{0,2,1:T(2,128)}), f32[4,8,2]{0,2,1:T(2,128)S(1)}, u32[]{:S(2)}, u32[]{:S(2)}) async-start(f32[4,8,2]{0,2,1:T(2,128)} %copy.18), calls=%async_computation.1 | async-start | bytes 16384 | tf_op jit(solution)/shard_map/all_to_all | solution.py:107
  39.4 40.5 %all-gather = bf16[32,4,512]{2,1,0:T(4,128)(2,1)S(1)} all-gather(bf16[1,4,512]{2,1,0:T(4,128)(2,1)S(1)} %bitcast.26), channel_id=1, replica_groups=mesh['role'=4,'dom'=8] {'role','dom'}, dimensions={0}, use_global_device_ids=true | all-gather | bytes 135168 | tf_op jit(solution)/shard_map/all_gather | solution.py:50
  80.0 2.0 %scatter_custom_fusion.2 = f32[64,512]{1,0:T(8,128)S(1)} fusion(s32[128]{0:T(128)S(1)} %fusion.19, f32[]{:T(128)} %constant.9.clone.1, bf16[128,512]{1,0:T(8,128)(2,1)S(1)} %copy-done.1, s32[1024]{0:T(1024)S(1)} %pad_clamp_fusion), kind=kCustom, calls=%fused_computation.23 | custom fusion | flops 131072 | bytes 266244 | tf_op jit(solution)/shard_map/scatter-add | solution.py:84
  81.9 0.7 reshape.178
  82.7 7.6 %scatter_custom_fusion.1 = f32[128]{0:T(128)S(1)} fusion(s32[1024]{0:T(1024)S(1)} %bitcast.28, f32[1024]{0:T(1024)S(1)} %broadcast.142, f32[]{:T(128)} %constant.9.clone.1), kind=kCustom, calls=%fused_computation.52 | custom fusion | flops 1024 | bytes 516 | tf_op jit(solution)/shard_map/while/body/eval_jaxpr/scatter-add | solution.py:63
  90.3 0.1 copy.24
  90.5 0.1 reshape.240
  90.6 0.0 all-to-all-done.1
  90.6 3.3 %all-to-all-start.2 = ((f32[4,8,2,512]{3,2,1,0:T(2,128)}), f32[4,8,2,512]{3,2,1,0:T(2,128)S(1)}, u32[]{:S(2)}, u32[]{:S(2)}) async-start(f32[4,8,2,512]{3,2,1,0:T(2,128)} %reshape.178), calls=%async_computation.2 | async-start | bytes 262144 | tf_op jit(solution)/shard_map/all_to_all | solution.py:94
  93.9 0.1 copy.19
  94.1 0.1 eq.15
  94.2 0.2 convolution_bitcast_fusion
  94.4 0.0 collective-permute-done
  94.4 0.0 collective-permute-done.1
  94.4 11.6 %scatter_custom_fusion = f32[128,512]{1,0:T(8,128)S(1)} fusion(s32[1024]{0:T(1024)S(1)} %bitcast.29, f32[]{:T(128)} %constant.9.clone.1, bf16[288,512]{1,0:T(8,128)(2,1)S(1)} %pad_maximum_fusion, s32[1024]{0:T(1024)S(1)} %broadcast_clamp_fusion), kind=kCustom, calls=%fused_computation.7 | custom fusion | flops 1048576 | bytes 561156 | tf_op jit(solution)/shard_map/while/body/eval_jaxpr/scatter-add | solution.py:63
  106.0 0.4 multiply_reduce_fusion
  106.4 0.0 all-to-all-done.2
  106.4 0.7 copy.20
  107.0 3.4 %all-to-all-start.3 = ((f32[4,8,2,512]{3,2,0,1:T(2,128)}), f32[4,8,2,512]{3,2,0,1:T(2,128)S(1)}, u32[]{:S(2)}, u32[]{:S(2)}) async-start(f32[4,8,2,512]{3,2,0,1:T(2,128)} %copy.20), calls=%async_computation.3 | async-start | bytes 262144 | tf_op jit(solution)/shard_map/all_to_all | solution.py:93
  110.4 0.7 multiply_convert_fusion
  111.2 5.9 %all-to-all-done.3 = f32[4,8,2,512]{3,2,0,1:T(2,128)S(1)} async-done(((f32[4,8,2,512]{3,2,0,1:T(2,128)}), f32[4,8,2,512]{3,2,0,1:T(2,128)S(1)}, u32[]{:S(2)}, u32[]{:S(2)}) %all-to-all-start.3) | async-done | bytes 131104 | tf_op jit(solution)/shard_map/all_to_all | solution.py:93
  117.1 0.1 reshape.179
  117.2 0.3 fusion.4
  117.5 0.3 multiply_reduce_fusion.1
  117.8 0.7 multiply_convert_fusion.1
  (25 shorter events, 0.2 us)
Async XLA Ops:
  0.6 15.4 %copy-start = (bf16[1024,512]{1,0:T(8,128)(2,1)S(1)}, bf16[1024,512]{1,0:T(8,128)(2,1)}, u32[]{:S(2)}) copy-start(bf16[1024,512]{1,0:T(8,128)(2,1)} %param.11) | copy-start | bytes 3145732
  0.6 79.3 %copy-start.1 = (bf16[128,512]{1,0:T(8,128)(2,1)S(1)}, bf16[128,512]{1,0:T(8,128)(2,1)}, u32[]{:S(2)}) copy-start(bf16[128,512]{1,0:T(8,128)(2,1)} %param.9) | copy-start | bytes 393220
  0.7 38.8 %copy-start.2 = (bf16[4,512]{1,0:T(4,128)(2,1)S(1)}, bf16[4,512]{1,0:T(4,128)(2,1)}, u32[]{:S(2)}) copy-start(bf16[4,512]{1,0:T(4,128)(2,1)} %param.10) | copy-start | bytes 12292
  0.7 16.2 %copy-start.3 = (s32[1,1024]{1,0:T(1,128)S(1)}, s32[1,1024]{1,0:T(1,128)}, u32[]{:S(2)}) copy-start(s32[1,1024]{1,0:T(1,128)} %param.13) | copy-start | bytes 12292
  0.7 16.2 %copy-start.4 = (s32[1,1024]{1,0:T(1,128)S(1)}, s32[1,1024]{1,0:T(1,128)}, u32[]{:S(2)}) copy-start(s32[1,1024]{1,0:T(1,128)} %param.12) | copy-start | bytes 12292
  0.7 16.2 %copy-start.5 = (s32[1,64]{1,0:T(1,128)S(1)}, s32[1,64]{1,0:T(1,128)}, u32[]{:S(2)}) copy-start(s32[1,64]{1,0:T(1,128)} %param.17) | copy-start | bytes 772
  0.7 21.9 %copy-start.6 = (s32[1,128]{1,0:T(1,128)S(1)}, s32[1,128]{1,0:T(1,128)}, u32[]{:S(2)}) copy-start(s32[1,128]{1,0:T(1,128)} %param.15) | copy-start | bytes 1540
  3.0 91.4 %collective-permute-start = (bf16[16,512]{1,0:T(8,128)(2,1)S(1)}, bf16[16,512]{1,0:T(8,128)(2,1)S(1)}, u32[]{:S(2)}, u32[]{:S(2)}) collective-permute-start(bf16[16,512]{1,0:T(8,128)(2,1)S(1)} %gather_fusion), channel_id=1, source_target_pairs={{0,1},{1,2},{2,3},{3,4},{4,5},{5,6},{6,7},{7,0},{8,9},{9,10},{10,1... | collective-permute-start | bytes 49160 | tf_op jit(solution)/shard_map/ppermute | solution.py:16
  3.5 90.9 %collective-permute-start.1 = (bf16[16,512]{1,0:T(8,128)(2,1)S(1)}, bf16[16,512]{1,0:T(8,128)(2,1)S(1)}, u32[]{:S(2)}, u32[]{:S(2)}) collective-permute-start(bf16[16,512]{1,0:T(8,128)(2,1)S(1)} %gather_fusion), channel_id=1, source_target_pairs={{1,0},{2,1},{3,2},{4,3},{5,4},{6,5},{7,6},{0,7},{9,8},{10,9},{11,1... | collective-permute-start | bytes 49160 | tf_op jit(solution)/shard_map/ppermute | solution.py:19
  10.5 8.8 %all-to-all-start.4 = ((f32[4,8,2]{1,2,0:T(2,128)}), f32[4,8,2]{1,2,0:T(2,128)S(1)}, u32[]{:S(2)}, u32[]{:S(2)}) async-start(f32[4,8,2]{1,2,0:T(2,128)} %copy.22), calls=%async_computation.4 | async-start | bytes 8192 | tf_op jit(solution)/shard_map/all_to_all | solution.py:101
  19.3 7.9 %all-to-all-start = ((f32[4,8,2]{1,2,0:T(2,128)}), f32[4,8,2]{1,2,0:T(2,128)S(1)}, u32[]{:S(2)}, u32[]{:S(2)}) async-start(f32[4,8,2]{1,2,0:T(2,128)} %copy.17), calls=%async_computation | async-start | bytes 8192 | tf_op jit(solution)/shard_map/all_to_all | solution.py:108
  27.2 8.9 %all-to-all-start.5 = ((f32[4,8,2]{0,2,1:T(2,128)}), f32[4,8,2]{0,2,1:T(2,128)S(1)}, u32[]{:S(2)}, u32[]{:S(2)}) async-start(f32[4,8,2]{0,2,1:T(2,128)} %copy.23), calls=%async_computation.5 | async-start | bytes 16384 | tf_op jit(solution)/shard_map/all_to_all | solution.py:100
  36.1 54.5 %all-to-all-start.1 = ((f32[4,8,2]{0,2,1:T(2,128)}), f32[4,8,2]{0,2,1:T(2,128)S(1)}, u32[]{:S(2)}, u32[]{:S(2)}) async-start(f32[4,8,2]{0,2,1:T(2,128)} %copy.18), calls=%async_computation.1 | async-start | bytes 16384 | tf_op jit(solution)/shard_map/all_to_all | solution.py:107
  90.6 15.8 %all-to-all-start.2 = ((f32[4,8,2,512]{3,2,1,0:T(2,128)}), f32[4,8,2,512]{3,2,1,0:T(2,128)S(1)}, u32[]{:S(2)}, u32[]{:S(2)}) async-start(f32[4,8,2,512]{3,2,1,0:T(2,128)} %reshape.178), calls=%async_computation.2 | async-start | bytes 262144 | tf_op jit(solution)/shard_map/all_to_all | solution.py:94
  107.0 10.1 %all-to-all-start.3 = ((f32[4,8,2,512]{3,2,0,1:T(2,128)}), f32[4,8,2,512]{3,2,0,1:T(2,128)S(1)}, u32[]{:S(2)}, u32[]{:S(2)}) async-start(f32[4,8,2,512]{3,2,0,1:T(2,128)} %copy.20), calls=%async_computation.3 | async-start | bytes 262144 | tf_op jit(solution)/shard_map/all_to_all | solution.py:93
where the time goes:
time: 119 us; the launch traced here: 118 us
  blocking collectives  40.5 us (34%)
  other arithmetic  25.5 us (21%)
  starting transfers between devices  25.4 us (21%)
  waiting for transfers between devices  16.3 us (14%)
  local copies, waits for them, and re-layouts  6.49 us (5%)
  matrix products  3.31 us (3%)
    all_gather x1, blocking collectives, on_device(): hub_table = lax.all_gather(hub_feats, ('role', 'dom'), axis=0, tiled=True)  40.5 us
    scatter-add x1, other arithmetic, add_block(): node_sums.at[block_targets].add(picked)  11.6 us
    scatter-add x1, other arithmetic, add_block(): node_degree.at[block_targets].add(1.0)  7.61 us
    all_to_all x1, waiting for transfers between devices, on_device(): lax.all_to_all(lax.all_to_all(outgoing[0], 'role', split_axis=0, concat_a...  5.94 us
    all_to_all x1, waiting for transfers between devices, on_device(): lax.all_to_all(lax.all_to_all(outgoing[1], 'role', split_axis=0, concat_a...  4.84 us
    all_to_all x1, starting transfers between devices, on_device(): lax.all_to_all(outgoing[1], 'role', split_axis=0, concat_axis=0, tiled=True)  4.15 us
    ppermute x1, starting transfers between devices, extended(): lax.ppermute(lax.slice_in_dim(block, 0, width, axis=dim), axis, backward)  4.09 us
    all_to_all x1, waiting for transfers between devices, on_device(): lax.all_to_all(outgoing[2], 'role', split_axis=0, concat_axis=0, tiled=True)  3.94 us
  transfers between devices with their start and end apart: 8, of which 4 were waited for; matrix products, arithmetic and copies ran while one was open for 26% of the time, Pallas kernels for 0%

commit v1 on v0

--- a/solution.py
+++ b/solution.py
@@ -47,7 +47,16 @@
     exports = node_feats[bound_rows[0]]
     bound_size = exports.shape[0]
     widened = extended(exports, (("dom", 0),), bound_size)
-    hub_table = lax.all_gather(hub_feats, ("role", "dom"), axis=0, tiled=True)
+    e_next, next_value = (lax.axis_size(("role", "dom")), lax.axis_index(("role", "dom")))
+    hub_table, odd = (hub_feats, 1)
+    while odd < e_next:
+        local_part = lax.ppermute(
+            hub_table, axis_name=("role", "dom"), perm=[(u, u ^ odd) for u in range(e_next)]
+        )
+        s_next = jnp.concatenate([hub_table, local_part], 0)
+        vec_out = jnp.concatenate([local_part, hub_table], 0)
+        hub_table = jnp.where(next_value & odd == 0, s_next, vec_out)
+        odd = 2 * odd
     source_table = jnp.concatenate(
         [node_feats, widened[:bound_size], widened[2 * bound_size :], hub_table], axis=0
     )

time: 119 us -> 82.2 us (0.69)
  blocking collectives: 40.5 us -> 0 us
  starting transfers between devices: 25.4 us -> 32.9 us
  waiting for transfers between devices: 16.3 us -> 13.1 us
    all_gather x1 -> x0, blocking collectives: 40.5 us -> none  [on_device(): hub_table = lax.all_gather(hub_feats, ('role', 'dom'), axis=0, tiled=True)]
    all_to_all x1, waiting for transfers between devices: 5.94 us -> 0.01 us  [on_device(): lax.all_to_all(lax.all_to_all(outgoing[0], 'role', split_axis=0, concat_a...]
    ppermute x0 -> x5, starting transfers between devices: none -> 5 us  [on_device(): lax.ppermute(hub_table, axis_name=('role', 'dom'), perm=[(u, u ^ odd) for...]
    ppermute x0 -> x5, waiting for transfers between devices: none -> 3.62 us  [on_device(): lax.ppermute(hub_table, axis_name=('role', 'dom'), perm=[(u, u ^ odd) for...]
    all_to_all x1, waiting for transfers between devices: 0.01 us -> 2.62 us  [on_device(): lax.all_to_all(outgoing[0], 'role', split_axis=0, concat_axis=0, tiled=True)]
    all_to_all x1, waiting for transfers between devices: 3.94 us -> 1.89 us  [on_device(): lax.all_to_all(outgoing[2], 'role', split_axis=0, concat_axis=0, tiled=True)]
    all_to_all x1, waiting for transfers between devices: 1.58 us -> 0.01 us  [on_device(): lax.all_to_all(outgoing[1], 'role', split_axis=0, concat_axis=0, tiled=True)]
    all_to_all x1, starting transfers between devices: 3.37 us -> 4.87 us  [on_device(): lax.all_to_all(lax.all_to_all(outgoing[0], 'role', split_axis=0, concat_a...]
  transfers between devices with their start and end apart: 8 -> 13, of which waited for: 4 -> 4; matrix products, arithmetic and copies ran while one was open for 26% -> 38% of each run, Pallas kernels for 0% -> 0%
where the time goes in v1:
time: 82.2 us; the launch traced here: 81.6 us
  starting transfers between devices  32.9 us (40%)
  other arithmetic  25.6 us (31%)
  waiting for transfers between devices  13.1 us (16%)
  local copies, waits for them, and re-layouts  6.46 us (8%)
  matrix products  2.62 us (3%)
  between operations  0.98 us (1%)
    scatter-add x1, other arithmetic, add_block(): node_sums.at[block_targets].add(picked)  11.6 us
    scatter-add x1, other arithmetic, add_block(): node_degree.at[block_targets].add(1.0)  7.61 us
    ppermute x5, starting transfers between devices, on_device(): lax.ppermute(hub_table, axis_name=('role', 'dom'), perm=[(u, u ^ odd) for...  5 us
    all_to_all x1, waiting for transfers between devices, on_device(): lax.all_to_all(lax.all_to_all(outgoing[1], 'role', split_axis=0, concat_a...  4.91 us
    all_to_all x1, starting transfers between devices, on_device(): lax.all_to_all(lax.all_to_all(outgoing[0], 'role', split_axis=0, concat_a...  4.87 us
    all_to_all x1, starting transfers between devices, on_device(): lax.all_to_all(outgoing[2], 'role', split_axis=0, concat_axis=0, tiled=True)  4.19 us
    all_to_all x1, starting transfers between devices, on_device(): lax.all_to_all(outgoing[1], 'role', split_axis=0, concat_axis=0, tiled=True)  4.15 us
    ppermute x1, starting transfers between devices, extended(): lax.ppermute(lax.slice_in_dim(block, 0, width, axis=dim), axis, backward)  4.09 us
  transfers between devices with their start and end apart: 13, of which 4 were waited for; matrix products, arithmetic and copies ran while one was open for 38% of the time, Pallas kernels for 0%

profile of v1, /device:TPU:0, one launch (start us, length us, event | category | flops | bytes accessed | tf_op | source)
XLA Modules:
  0.0 81.6 jit_solution(15342850252344674569)
XLA Ops:
  0.6 0.0 copy-start.2
  0.6 0.0 copy-start
  0.7 0.0 copy-start.1
  0.7 0.7 fusion.18
  1.5 1.5 %gather_fusion = bf16[16,512]{1,0:T(8,128)(2,1)S(1)} fusion(bf16[128,512]{1,0:T(8,128)(2,1)} %param.9, s32[1024]{0:T(1024)S(1)} %pad_clamp_fusion.1), kind=kCustom, calls=%fused_computation | custom fusion | bytes 32832 | tf_op jit(solution)/shard_map/gather | solution.py:47
  3.0 0.5 collective-permute-start
  3.5 4.1 %collective-permute-start.1 = (bf16[16,512]{1,0:T(8,128)(2,1)S(1)}, bf16[16,512]{1,0:T(8,128)(2,1)S(1)}, u32[]{:S(2)}, u32[]{:S(2)}) collective-permute-start(bf16[16,512]{1,0:T(8,128)(2,1)S(1)} %gather_fusion), channel_id=1, source_target_pairs={{1,0},{2,1},{3,2},{4,3},{5,4},{6,5},{7,6},{0,7},{9,8},{10,9},{11,1... | collective-permute-start | bytes 49160 | tf_op jit(solution)/shard_map/ppermute | solution.py:19
  7.6 0.0 collective-permute-start.2
  7.6 0.7 fusion.19
  8.3 1.4 %scatter_custom_fusion.3 = f32[64]{0:T(128)S(1)} fusion(s32[128]{0:T(128)S(1)} %fusion.19, f32[128]{0:T(128)S(1)} %broadcast.143, f32[]{:T(128)} %constant.15.clone.1), kind=kCustom, calls=%fused_computation.55 | custom fusion | flops 128 | bytes 260 | tf_op jit(solution)/shard_map/scatter-add | solution.py:95
  9.7 0.1 reshape.180
  9.8 0.7 copy.22
  10.5 4.2 %all-to-all-start.4 = ((f32[4,8,2]{1,2,0:T(2,128)}), f32[4,8,2]{1,2,0:T(2,128)S(1)}, u32[]{:S(2)}, u32[]{:S(2)}) async-start(f32[4,8,2]{1,2,0:T(2,128)} %copy.22), calls=%async_computation.4 | async-start | bytes 8192 | tf_op jit(solution)/shard_map/all_to_all | solution.py:110
  14.6 1.3 %fusion.9 = f32[128,512]{1,0:T(8,128)S(1)} fusion(bf16[128,512]{1,0:T(8,128)(2,1)} %param.9, bf16[1024,512]{1,0:T(8,128)(2,1)} %param.11), kind=kOutput, calls=%fused_computation.20 | convolution fusion | flops 67108864 | bytes 917504 | tf_op jit(solution)/shard_map/dot_general | solution.py:26
  16.0 0.2 fusion.7
  16.3 0.1 collective-permute-start.3
  16.4 3.6 %collective-permute-done.3 = bf16[8,512]{1,0:T(8,128)(2,1)S(1)} collective-permute-done((bf16[8,512]{1,0:T(8,128)(2,1)S(1)}, bf16[8,512]{1,0:T(8,128)(2,1)S(1)}, u32[]{:S(2)}, u32[]{:S(2)}) %collective-permute-start.3) | collective-permute-done | bytes 8224 | tf_op jit(solution)/shard_map/ppermute | solution.py:53
  20.0 0.8 collective-permute-start.4
  20.8 0.1 convert_element_type.31
  20.9 0.7 copy.17
  21.6 4.2 %all-to-all-start = ((f32[4,8,2]{1,2,0:T(2,128)}), f32[4,8,2]{1,2,0:T(2,128)S(1)}, u32[]{:S(2)}, u32[]{:S(2)}) async-start(f32[4,8,2]{1,2,0:T(2,128)} %copy.17), calls=%async_computation | async-start | bytes 8192 | tf_op jit(solution)/shard_map/all_to_all | solution.py:117
  25.8 0.7 copy.23
  26.5 2.1 %collective-permute-start.5 = (bf16[32,512]{1,0:T(8,128)(2,1)S(1)}, bf16[32,512]{1,0:T(8,128)(2,1)S(1)}, u32[]{:S(2)}, u32[]{:S(2)}) collective-permute-start(bf16[32,512]{1,0:T(8,128)(2,1)S(1)} %maximum_select_fusion.2), channel_id=1, source_target_pairs={{0,8},{1,9},{2,10},{3,11},{4,12},{5,13},{6,14},{7,15},{8,0},{9,1},... | collective-permute-start | bytes 98312 | tf_op jit(solution)/shard_map/ppermute | solution.py:53
  28.6 1.9 %all-to-all-done = f32[4,8,2]{1,2,0:T(2,128)S(1)} async-done(((f32[4,8,2]{1,2,0:T(2,128)}), f32[4,8,2]{1,2,0:T(2,128)S(1)}, u32[]{:S(2)}, u32[]{:S(2)}) %all-to-all-start) | async-done | bytes 288 | tf_op jit(solution)/shard_map/all_to_all | solution.py:117
  30.5 3.4 %all-to-all-start.5 = ((f32[4,8,2]{0,2,1:T(2,128)}), f32[4,8,2]{0,2,1:T(2,128)S(1)}, u32[]{:S(2)}, u32[]{:S(2)}) async-start(f32[4,8,2]{0,2,1:T(2,128)} %copy.23), calls=%async_computation.5 | async-start | bytes 16384 | tf_op jit(solution)/shard_map/all_to_all | solution.py:109
  33.9 0.7 copy.18
  34.6 4.9 %all-to-all-done.5 = f32[4,8,2]{0,2,1:T(2,128)S(1)} async-done(((f32[4,8,2]{0,2,1:T(2,128)}), f32[4,8,2]{0,2,1:T(2,128)S(1)}, u32[]{:S(2)}, u32[]{:S(2)}) %all-to-all-start.5) | async-done | bytes 288 | tf_op jit(solution)/shard_map/all_to_all | solution.py:109
  39.5 3.3 %all-to-all-start.1 = ((f32[4,8,2]{0,2,1:T(2,128)}), f32[4,8,2]{0,2,1:T(2,128)S(1)}, u32[]{:S(2)}, u32[]{:S(2)}) async-start(f32[4,8,2]{0,2,1:T(2,128)} %copy.18), calls=%async_computation.1 | async-start | bytes 16384 | tf_op jit(solution)/shard_map/all_to_all | solution.py:116
  42.9 2.0 %scatter_custom_fusion.2 = f32[64,512]{1,0:T(8,128)S(1)} fusion(s32[128]{0:T(128)S(1)} %fusion.19, f32[]{:T(128)} %constant.15.clone.1, bf16[128,512]{1,0:T(8,128)(2,1)S(1)} %copy-done.1, s32[1024]{0:T(1024)S(1)} %pad_clamp_fusion), kind=kCustom, calls=%fused_computation.23 | custom fusion | flops 131072 | bytes 266244 | tf_op jit(solution)/shard_map/scatter-add | solution.py:93
  44.8 0.7 reshape.178
  45.5 7.6 %scatter_custom_fusion.1 = f32[128]{0:T(128)S(1)} fusion(s32[1024]{0:T(1024)S(1)} %bitcast.26, f32[1024]{0:T(1024)S(1)} %broadcast.142, f32[]{:T(128)} %constant.15.clone.1), kind=kCustom, calls=%fused_computation.57 | custom fusion | flops 1024 | bytes 516 | tf_op jit(solution)/shard_map/while/body/eval_jaxpr/scatter-add | solution.py:72
  53.2 0.1 copy.24
  53.3 0.1 reshape.238
  53.4 3.3 %all-to-all-start.2 = ((f32[4,8,2,512]{3,2,1,0:T(2,128)}), f32[4,8,2,512]{3,2,1,0:T(2,128)S(1)}, u32[]{:S(2)}, u32[]{:S(2)}) async-start(f32[4,8,2,512]{3,2,1,0:T(2,128)} %reshape.178), calls=%async_computation.2 | async-start | bytes 262144 | tf_op jit(solution)/shard_map/all_to_all | solution.py:103
  56.8 0.1 copy.19
  56.9 0.1 eq.35
  57.0 2.1 %collective-permute-start.6 = (bf16[64,512]{1,0:T(8,128)(2,1)S(1)}, bf16[64,512]{1,0:T(8,128)(2,1)S(1)}, u32[]{:S(2)}, u32[]{:S(2)}) collective-permute-start(bf16[64,512]{1,0:T(8,128)(2,1)S(1)} %maximum_select_fusion.1), channel_id=1, source_target_pairs={{0,16},{1,17},{2,18},{3,19},{4,20},{5,21},{6,22},{7,23},{8,24},{9,... | collective-permute-start | bytes 196616 | tf_op jit(solution)/shard_map/ppermute | solution.py:53
  59.1 0.2 convolution_bitcast_fusion
  59.3 2.6 %all-to-all-done.2 = f32[4,8,2,512]{3,2,1,0:T(2,128)S(1)} async-done(((f32[4,8,2,512]{3,2,1,0:T(2,128)}), f32[4,8,2,512]{3,2,1,0:T(2,128)S(1)}, u32[]{:S(2)}, u32[]{:S(2)}) %all-to-all-start.2) | async-done | bytes 131104 | tf_op jit(solution)/shard_map/all_to_all | solution.py:103
  61.9 0.7 copy.20
  62.6 4.9 %all-to-all-start.3 = ((f32[4,8,2,512]{3,2,0,1:T(2,128)}), f32[4,8,2,512]{3,2,0,1:T(2,128)S(1)}, u32[]{:S(2)}, u32[]{:S(2)}) async-start(f32[4,8,2,512]{3,2,0,1:T(2,128)} %copy.20), calls=%async_computation.3 | async-start | bytes 262144 | tf_op jit(solution)/shard_map/all_to_all | solution.py:102
  67.5 11.6 %scatter_custom_fusion = f32[128,512]{1,0:T(8,128)S(1)} fusion(s32[1024]{0:T(1024)S(1)} %bitcast.27, f32[]{:T(128)} %constant.15.clone.1, bf16[288,512]{1,0:T(8,128)(2,1)S(1)} %pad_maximum_fusion, s32[1024]{0:T(1024)S(1)} %broadcast_clamp_fusion), kind=kCustom, calls=%fused_computation.7 | custom fusion | flops 1048576 | bytes 561156 | tf_op jit(solution)/shard_map/while/body/eval_jaxpr/scatter-add | solution.py:72
  79.1 0.4 multiply_reduce_fusion
  79.5 0.8 multiply_convert_fusion
  80.2 0.1 reshape.179
  80.3 0.3 fusion.4
  80.6 0.3 multiply_reduce_fusion.1
  80.9 0.7 multiply_convert_fusion.1
  (38 shorter events, 0.2 us)
Async XLA Ops:
  0.6 15.4 %copy-start.2 = (bf16[4,512]{1,0:T(4,128)(2,1)S(1)}, bf16[4,512]{1,0:T(4,128)(2,1)}, u32[]{:S(2)}) copy-start(bf16[4,512]{1,0:T(4,128)(2,1)} %param.10) | copy-start | bytes 12292
  0.6 15.4 %copy-start = (bf16[1024,512]{1,0:T(8,128)(2,1)S(1)}, bf16[1024,512]{1,0:T(8,128)(2,1)}, u32[]{:S(2)}) copy-start(bf16[1024,512]{1,0:T(8,128)(2,1)} %param.11) | copy-start | bytes 3145732
  0.7 42.2 %copy-start.1 = (bf16[128,512]{1,0:T(8,128)(2,1)S(1)}, bf16[128,512]{1,0:T(8,128)(2,1)}, u32[]{:S(2)}) copy-start(bf16[128,512]{1,0:T(8,128)(2,1)} %param.9) | copy-start | bytes 393220
  0.7 15.5 %copy-start.3 = (s32[1,1024]{1,0:T(1,128)S(1)}, s32[1,1024]{1,0:T(1,128)}, u32[]{:S(2)}) copy-start(s32[1,1024]{1,0:T(1,128)} %param.13) | copy-start | bytes 12292
  0.7 15.5 %copy-start.4 = (s32[1,1024]{1,0:T(1,128)S(1)}, s32[1,1024]{1,0:T(1,128)}, u32[]{:S(2)}) copy-start(s32[1,1024]{1,0:T(1,128)} %param.12) | copy-start | bytes 12292
  0.7 15.7 %copy-start.5 = (s32[1,128]{1,0:T(1,128)S(1)}, s32[1,128]{1,0:T(1,128)}, u32[]{:S(2)}) copy-start(s32[1,128]{1,0:T(1,128)} %param.15) | copy-start | bytes 1540
  0.7 20.1 %copy-start.6 = (s32[1,64]{1,0:T(1,128)S(1)}, s32[1,64]{1,0:T(1,128)}, u32[]{:S(2)}) copy-start(s32[1,64]{1,0:T(1,128)} %param.17) | copy-start | bytes 772
  3.0 64.5 %collective-permute-start = (bf16[16,512]{1,0:T(8,128)(2,1)S(1)}, bf16[16,512]{1,0:T(8,128)(2,1)S(1)}, u32[]{:S(2)}, u32[]{:S(2)}) collective-permute-start(bf16[16,512]{1,0:T(8,128)(2,1)S(1)} %gather_fusion), channel_id=1, source_target_pairs={{0,1},{1,2},{2,3},{3,4},{4,5},{5,6},{6,7},{7,0},{8,9},{9,10},{10,1... | collective-permute-start | bytes 49160 | tf_op jit(solution)/shard_map/ppermute | solution.py:16
  3.5 64.0 %collective-permute-start.1 = (bf16[16,512]{1,0:T(8,128)(2,1)S(1)}, bf16[16,512]{1,0:T(8,128)(2,1)S(1)}, u32[]{:S(2)}, u32[]{:S(2)}) collective-permute-start(bf16[16,512]{1,0:T(8,128)(2,1)S(1)} %gather_fusion), channel_id=1, source_target_pairs={{1,0},{2,1},{3,2},{4,3},{5,4},{6,5},{7,6},{0,7},{9,8},{10,9},{11,1... | collective-permute-start | bytes 49160 | tf_op jit(solution)/shard_map/ppermute | solution.py:19
  7.6 8.6 %collective-permute-start.2 = (bf16[4,512]{1,0:T(4,128)(2,1)}, bf16[4,512]{1,0:T(4,128)(2,1)S(1)}, u32[]{:S(2)}, u32[]{:S(2)}) collective-permute-start(bf16[4,512]{1,0:T(4,128)(2,1)} %param.10), channel_id=1, source_target_pairs={{0,1},{1,0},{2,3},{3,2},{4,5},{5,4},{6,7},{7,6},{8,9},{9,8},{10,11... | collective-permute-start | bytes 12296 | tf_op jit(solution)/shard_map/ppermute | solution.py:53
  10.5 11.1 %all-to-all-start.4 = ((f32[4,8,2]{1,2,0:T(2,128)}), f32[4,8,2]{1,2,0:T(2,128)S(1)}, u32[]{:S(2)}, u32[]{:S(2)}) async-start(f32[4,8,2]{1,2,0:T(2,128)} %copy.22), calls=%async_computation.4 | async-start | bytes 8192 | tf_op jit(solution)/shard_map/all_to_all | solution.py:110
  16.3 3.7 %collective-permute-start.3 = (bf16[8,512]{1,0:T(8,128)(2,1)S(1)}, bf16[8,512]{1,0:T(8,128)(2,1)S(1)}, u32[]{:S(2)}, u32[]{:S(2)}) collective-permute-start(bf16[8,512]{1,0:T(8,128)(2,1)S(1)} %maximum_select_fusion.4), channel_id=1, source_target_pairs={{0,2},{1,3},{2,0},{3,1},{4,6},{5,7},{6,4},{7,5},{8,10},{9,11},{10,... | collective-permute-start | bytes 24584 | tf_op jit(solution)/shard_map/ppermute | solution.py:53
  20.0 6.5 %collective-permute-start.4 = (bf16[16,512]{1,0:T(8,128)(2,1)S(1)}, bf16[16,512]{1,0:T(8,128)(2,1)S(1)}, u32[]{:S(2)}, u32[]{:S(2)}) collective-permute-start(bf16[16,512]{1,0:T(8,128)(2,1)S(1)} %maximum_select_fusion.3), channel_id=1, source_target_pairs={{0,4},{1,5},{2,6},{3,7},{4,0},{5,1},{6,2},{7,3},{8,12},{9,13},{10,... | collective-permute-start | bytes 49160 | tf_op jit(solution)/shard_map/ppermute | solution.py:53
  21.6 8.9 %all-to-all-start = ((f32[4,8,2]{1,2,0:T(2,128)}), f32[4,8,2]{1,2,0:T(2,128)S(1)}, u32[]{:S(2)}, u32[]{:S(2)}) async-start(f32[4,8,2]{1,2,0:T(2,128)} %copy.17), calls=%async_computation | async-start | bytes 8192 | tf_op jit(solution)/shard_map/all_to_all | solution.py:117
  26.5 30.5 %collective-permute-start.5 = (bf16[32,512]{1,0:T(8,128)(2,1)S(1)}, bf16[32,512]{1,0:T(8,128)(2,1)S(1)}, u32[]{:S(2)}, u32[]{:S(2)}) collective-permute-start(bf16[32,512]{1,0:T(8,128)(2,1)S(1)} %maximum_select_fusion.2), channel_id=1, source_target_pairs={{0,8},{1,9},{2,10},{3,11},{4,12},{5,13},{6,14},{7,15},{8,0},{9,1},... | collective-permute-start | bytes 98312 | tf_op jit(solution)/shard_map/ppermute | solution.py:53
  30.5 9.0 %all-to-all-start.5 = ((f32[4,8,2]{0,2,1:T(2,128)}), f32[4,8,2]{0,2,1:T(2,128)S(1)}, u32[]{:S(2)}, u32[]{:S(2)}) async-start(f32[4,8,2]{0,2,1:T(2,128)} %copy.23), calls=%async_computation.5 | async-start | bytes 16384 | tf_op jit(solution)/shard_map/all_to_all | solution.py:109
  39.5 13.9 %all-to-all-start.1 = ((f32[4,8,2]{0,2,1:T(2,128)}), f32[4,8,2]{0,2,1:T(2,128)S(1)}, u32[]{:S(2)}, u32[]{:S(2)}) async-start(f32[4,8,2]{0,2,1:T(2,128)} %copy.18), calls=%async_computation.1 | async-start | bytes 16384 | tf_op jit(solution)/shard_map/all_to_all | solution.py:116
  53.4 8.5 %all-to-all-start.2 = ((f32[4,8,2,512]{3,2,1,0:T(2,128)}), f32[4,8,2,512]{3,2,1,0:T(2,128)S(1)}, u32[]{:S(2)}, u32[]{:S(2)}) async-start(f32[4,8,2,512]{3,2,1,0:T(2,128)} %reshape.178), calls=%async_computation.2 | async-start | bytes 262144 | tf_op jit(solution)/shard_map/all_to_all | solution.py:103
  57.0 10.4 %collective-permute-start.6 = (bf16[64,512]{1,0:T(8,128)(2,1)S(1)}, bf16[64,512]{1,0:T(8,128)(2,1)S(1)}, u32[]{:S(2)}, u32[]{:S(2)}) collective-permute-start(bf16[64,512]{1,0:T(8,128)(2,1)S(1)} %maximum_select_fusion.1), channel_id=1, source_target_pairs={{0,16},{1,17},{2,18},{3,19},{4,20},{5,21},{6,22},{7,23},{8,24},{9,... | collective-permute-start | bytes 196616 | tf_op jit(solution)/shard_map/ppermute | solution.py:53
  62.6 17.7 %all-to-all-start.3 = ((f32[4,8,2,512]{3,2,0,1:T(2,128)}), f32[4,8,2,512]{3,2,0,1:T(2,128)S(1)}, u32[]{:S(2)}, u32[]{:S(2)}) async-start(f32[4,8,2,512]{3,2,0,1:T(2,128)} %copy.20), calls=%async_computation.3 | async-start | bytes 262144 | tf_op jit(solution)/shard_map/all_to_all | solution.py:102
